TPU v7x, 128 devices: a whole 4x4x4 slice. The times are simulated.
128 devices in a mesh: dp: 16 (over x_lo, y, core), tensor: 8 (over x_hi, z).
Axes of the slice: x: 4 (x_hi: 2, x_lo: 2; x = x_hi * 2 + x_lo), y: 4, z: 4, core: 2. Of those that a mesh axis runs over, the one named last changes fastest.
Arguments:
- block_input: bfloat16 [32768, 768], P(('dp', 'tensor')), may hold values from -6 to 6
- w_value: bfloat16 [768, 768], replicated, may hold values from -0.21875 to 0.21875
- b_value: bfloat16 [768], replicated, may hold values from -2 to 2
- conv_kernel: bfloat16 [65, 768], replicated, may hold values from -0.75 to 0.75
- w_out: bfloat16 [768, 768], replicated, may hold values from -0.21875 to 0.21875
- b_out: bfloat16 [768], replicated, may hold values from -2 to 2
- gain_attn: bfloat16 [768], replicated, may hold values from 0.5 to 1.5
- shift_attn: bfloat16 [768], replicated, may hold values from -2 to 2
- w_up: bfloat16 [768, 3072], P(None, 'tensor'), may hold values from -0.21875 to 0.21875
- b_up: bfloat16 [3072], P('tensor'), may hold values from -2 to 2
- w_down: bfloat16 [3072, 768], P('tensor'), may hold values from -0.109375 to 0.109375
- b_down: bfloat16 [768], replicated, may hold values from -2 to 2
- gain_ffn: bfloat16 [768], replicated, may hold values from 0.5 to 1.5
- shift_ffn: bfloat16 [768], replicated, may hold values from -2 to 2
- query_codes: int32 [32768, 384], P(('dp', 'tensor')), may hold values from 0 to 255
- key_codes: int32 [32768, 384], P(('dp', 'tensor')), may hold values from 0 to 255
- key_live: int32 [32768], P(('dp', 'tensor')), may hold values 0 or 1
- seq_lengths: int32 [128, 4], P(('dp', 'tensor')), may hold values from 1 to 128, 256 in all within a row
- out_grad: bfloat16 [32768, 768], P(('dp', 'tensor')), may hold values from -6 to 6
Outputs:
- block_output: bfloat16 [32768, 768], P(('dp', 'tensor'))
- input_grad: float32 [32768, 768], P(('dp', 'tensor'))
- grad_w_value: float32 [768, 768], replicated
- grad_b_value: float32 [768], replicated
- grad_conv_kernel: float32 [65, 768], replicated
- grad_w_out: float32 [768, 768], replicated
- grad_b_out: float32 [768], replicated
- grad_gain_attn: float32 [768], replicated
- grad_shift_attn: float32 [768], replicated
- grad_w_up: float32 [768, 3072], P(None, 'tensor')
- grad_b_up: float32 [3072], P('tensor')
- grad_w_down: float32 [3072, 768], P('tensor')
- grad_b_down: float32 [768], replicated
- grad_gain_ffn: float32 [768], replicated
- grad_shift_ffn: float32 [768], replicated
Inputs may be any that keep to these rules, and one draw needn't show every extreme that they name: `seq_lengths`: each item's lengths sum to 256; the longest is 128. `key_live`: 1 marks a live key, 0 a padded one. `query_codes`: column h * 32 + s holds head h's code in hash set s. `key_codes`: column h * 32 + s holds head h's code in hash set s.
All inputs are finite; a program needn't handle non-finite values. No bound on the sum of `key_live` on one device may be relied on, other than what follows from the above.
Results may differ from a plain program's by a relative error of at most 0.02.
Values may be sent and summed in bfloat16 or wider, within the bound.
No kernel may reach another device: no remote copies, remote signals or barrier semaphores. Data moves between devices by JAX's collectives and lax.ppermute only.
A program may use at most 128 MiB of HBM per device.

v0:
```python
from functools import partial
import jax
import jax.numpy as jnp
from jax import lax
from jax.sharding import PartitionSpec as P

HEADS = 12
SETS = 32
BUCKETS = 256


def dot_last(former, latter):
    return lax.dot_general(
        former, latter, (((1,), (1,)), ((), ())), preferred_element_type=jnp.float32
    )


def dot_first(former, latter):
    return lax.dot_general(
        former, latter, (((0,), (0,)), ((), ())), preferred_element_type=jnp.float32
    )


def layer_norm(residual, gain_vec, shift_vec):
    average = jnp.mean(residual, axis=-1, keepdims=True)
    centred = residual - average
    variance = jnp.mean(centred * centred, axis=-1, keepdims=True)
    return centred * lax.rsqrt(variance + 1e-05) * gain_vec + shift_vec


def head_norm(mixed, head_count, head_dim):
    grouped = mixed.reshape(mixed.shape[0], head_count, head_dim)
    scaling = lax.rsqrt(jnp.mean(grouped * grouped, axis=-1, keepdims=True) + 1e-06)
    return (grouped * scaling).reshape(mixed.shape)


def gelu_exact(pre_act):
    return jax.nn.gelu(pre_act, approximate=False)


def depth_conv(values, kernel, segment):
    taps = kernel.shape[0]
    margin = taps // 2
    length = values.shape[0]
    padded = jnp.pad(values, ((margin, margin), (0, 0)))
    seg_padded = jnp.pad(segment, (margin, margin), constant_values=-1)
    running = jnp.zeros_like(values)
    for offset in range(taps):
        joined = (seg_padded[offset : offset + length] == segment).astype(jnp.float32)[:, None]
        running = running + padded[offset : offset + length] * joined * kernel[offset][None, :]
    return running


def conv_back(grad_out, values, kernel, segment):
    taps = kernel.shape[0]
    margin = taps // 2
    length = values.shape[0]
    padded = jnp.pad(values, ((margin, margin), (0, 0)))
    grad_padded = jnp.pad(grad_out, ((margin, margin), (0, 0)))
    seg_padded = jnp.pad(segment, (margin, margin), constant_values=-1)
    value_grad = jnp.zeros_like(values)
    tap_rows = []
    for offset in range(taps):
        joined = (seg_padded[offset : offset + length] == segment).astype(jnp.float32)[:, None]
        tap_rows.append(jnp.sum(grad_out * joined * padded[offset : offset + length], axis=0))
        mirror = 2 * margin - offset
        back_joined = (seg_padded[mirror : mirror + length] == segment).astype(jnp.float32)[:, None]
        value_grad = (
            value_grad
            + grad_padded[mirror : mirror + length] * back_joined * kernel[offset][None, :]
        )
    return (value_grad, jnp.stack(tap_rows, axis=0))


def body(
    block_input,
    w_value,
    b_value,
    conv_kernel,
    w_out,
    b_out,
    gain_attn,
    shift_attn,
    w_up,
    b_up,
    w_down,
    b_down,
    gain_ffn,
    shift_ffn,
    query_codes,
    key_codes,
    key_live,
    seq_lengths,
    out_grad,
):
    length = block_input.shape[0]
    model_width = block_input.shape[1]
    head_dim = model_width // HEADS
    live_keys = key_live.astype(jnp.float32)[:, None]
    seq_ends = jnp.cumsum(seq_lengths[0], dtype=jnp.int32)
    positions = jnp.arange(length, dtype=jnp.int32)
    segment = jnp.sum(
        (seq_ends[None, :] <= positions[:, None]).astype(jnp.int32), axis=1, dtype=jnp.int32
    )
    query_heads = query_codes.reshape(length, HEADS, SETS).transpose(1, 0, 2)
    key_heads = key_codes.reshape(length, HEADS, SETS).transpose(1, 0, 2)
    joined = (segment[:, None] == segment[None, :]).astype(jnp.float32)
    bucket_ids = jnp.arange(BUCKETS, dtype=jnp.int32)

    def head_counts(pair):
        query_set, key_set = pair
        query_hot = (
            (query_set[:, :, None] == bucket_ids[None, None, :])
            .astype(jnp.bfloat16)
            .reshape(length, SETS * BUCKETS)
        )
        key_hot = (
            (key_set[:, :, None] == bucket_ids[None, None, :])
            .astype(jnp.bfloat16)
            .reshape(length, SETS * BUCKETS)
        )
        counts = dot_last(query_hot, key_hot)
        return (counts * joined / SETS).astype(jnp.bfloat16)

    collide = lax.map(head_counts, (query_heads, key_heads))
    kernel_f = conv_kernel.astype(jnp.float32)
    value_pre = jnp.dot(block_input, w_value, preferred_element_type=jnp.float32) + b_value.astype(
        jnp.float32
    )
    values = value_pre.astype(jnp.bfloat16)
    masked = values.astype(jnp.float32) * live_keys
    masked_low = masked.astype(jnp.bfloat16)
    mixed = jnp.einsum(
        "hij,jhd->ihd",
        collide,
        masked_low.reshape(length, HEADS, head_dim),
        preferred_element_type=jnp.float32,
    ).reshape(length, model_width)
    normed, norm_back = jax.vjp(partial(head_norm, head_count=HEADS, head_dim=head_dim), mixed)
    context = (normed + depth_conv(masked, kernel_f, segment)).astype(jnp.bfloat16)
    attended = jnp.dot(context, w_out, preferred_element_type=jnp.float32) + b_out.astype(
        jnp.float32
    )
    first, first_back = jax.vjp(
        layer_norm,
        block_input.astype(jnp.float32) + attended,
        gain_attn.astype(jnp.float32),
        shift_attn.astype(jnp.float32),
    )
    first_low = first.astype(jnp.bfloat16)
    gathered = lax.all_gather(first_low, "tensor", axis=0, tiled=True)
    upper = jnp.dot(gathered, w_up, preferred_element_type=jnp.float32) + b_up.astype(jnp.float32)
    active_f, gelu_back = jax.vjp(gelu_exact, upper)
    active = active_f.astype(jnp.bfloat16)
    branch = lax.psum_scatter(
        jnp.dot(active, w_down, preferred_element_type=jnp.float32).astype(jnp.bfloat16),
        "tensor",
        scatter_dimension=0,
        tiled=True,
    ).astype(jnp.float32) + b_down.astype(jnp.float32)
    block_output, second_back = jax.vjp(
        layer_norm, first + branch, gain_ffn.astype(jnp.float32), shift_ffn.astype(jnp.float32)
    )
    grad_second, grad_gain_ffn, grad_shift_ffn = second_back(out_grad.astype(jnp.float32))
    branch_grad = grad_second.astype(jnp.bfloat16)
    grad_b_down = jnp.sum(branch_grad.astype(jnp.float32), axis=0)
    grad_rows_all = lax.all_gather(branch_grad, "tensor", axis=0, tiled=True)
    active_grad = dot_last(grad_rows_all, w_down)
    grad_w_down = dot_first(active, grad_rows_all)
    upper_grad = gelu_back(active_grad)[0].astype(jnp.bfloat16)
    grad_w_up = dot_first(gathered, upper_grad)
    grad_b_up = jnp.sum(upper_grad.astype(jnp.float32), axis=0)
    first_grad_ffn = lax.psum_scatter(
        dot_last(upper_grad, w_up).astype(jnp.bfloat16), "tensor", scatter_dimension=0, tiled=True
    ).astype(jnp.float32)
    first_grad = grad_second + first_grad_ffn
    resid_grad, grad_gain_attn, grad_shift_attn = first_back(first_grad)
    attended_grad = resid_grad.astype(jnp.bfloat16)
    grad_b_out = jnp.sum(attended_grad.astype(jnp.float32), axis=0)
    grad_w_out = dot_first(context, attended_grad)
    context_grad = dot_last(attended_grad, w_out)
    mixed_grad = norm_back(context_grad)[0].astype(jnp.bfloat16)
    conv_value_grad, grad_kernel = conv_back(context_grad, masked, kernel_f, segment)
    masked_att = jnp.einsum(
        "hij,ihd->jhd",
        collide,
        mixed_grad.reshape(length, HEADS, head_dim),
        preferred_element_type=jnp.float32,
    ).reshape(length, model_width)
    value_grad = ((masked_att + conv_value_grad) * live_keys).astype(jnp.bfloat16)
    grad_b_value = jnp.sum(value_grad.astype(jnp.float32), axis=0)
    grad_w_value = dot_first(block_input, value_grad)
    input_grad = resid_grad + dot_last(value_grad, w_value)
    grad_w_up, grad_w_down, grad_b_up = (
        lax.psum(grad_w_up.astype(jnp.bfloat16), "dp").astype(jnp.float32),
        lax.psum(grad_w_down.astype(jnp.bfloat16), "dp").astype(jnp.float32),
        lax.psum(grad_b_up.astype(jnp.bfloat16), "dp").astype(jnp.float32),
    )
    (
        grad_w_value,
        grad_b_value,
        grad_kernel,
        grad_w_out,
        grad_b_out,
        grad_gain_attn,
        grad_shift_attn,
        grad_b_down,
        grad_gain_ffn,
        grad_shift_ffn,
    ) = lax.psum(
        (
            grad_w_value,
            grad_b_value,
            grad_kernel,
            grad_w_out,
            grad_b_out,
            grad_gain_attn,
            grad_shift_attn,
            grad_b_down,
            grad_gain_ffn,
            grad_shift_ffn,
        ),
        ("dp", "tensor"),
    )
    return (
        block_output.astype(jnp.bfloat16),
        input_grad,
        grad_w_value,
        grad_b_value,
        grad_kernel,
        grad_w_out,
        grad_b_out,
        grad_gain_attn,
        grad_shift_attn,
        grad_w_up,
        grad_b_up,
        grad_w_down,
        grad_b_down,
        grad_gain_ffn,
        grad_shift_ffn,
    )


def solution(mesh):
    return jax.shard_map(
        body,
        mesh=mesh,
        in_specs=(
            P(("dp", "tensor"), None),
            P(),
            P(),
            P(),
            P(),
            P(),
            P(),
            P(),
            P(None, "tensor"),
            P("tensor"),
            P("tensor", None),
            P(),
            P(),
            P(),
            P(("dp", "tensor"), None),
            P(("dp", "tensor"), None),
            P(("dp", "tensor")),
            P(("dp", "tensor"), None),
            P(("dp", "tensor"), None),
        ),
        out_specs=(
            P(("dp", "tensor"), None),
            P(("dp", "tensor"), None),
            P(),
            P(),
            P(),
            P(),
            P(),
            P(),
            P(),
            P(None, "tensor"),
            P("tensor"),
            P("tensor", None),
            P(),
            P(),
            P(),
        ),
        check_vma=False,
    )
```

profile of v0, /device:TPU:1, one launch (start us, length us, event | category | flops | bytes accessed | tf_op | source)
XLA Modules:
  0.0 701.4 jit_solution(10940862884612107198)
XLA Ops:
  17.3 43.1 %while.12 = (s32[]{:T(128)}, bf16[12,256,256]{2,1,0:T(8,128)(2,1)}, s32[12,256,32]{1,2,0:T(8,128)S(1)}, s32[12,256,32]{1,2,0:T(8,128)S(1)}, s32[256]{0:T(256)S(1)}, /*index=5*/s32[]{:T(128)}) while((s32[]{:T(128)}, bf16[12,256,256]{2,1,0:T(8,128)(2,1)}, s32[12,256,32]{1,2,0:T(8,128)S(1)}, s32[12,256,32]{1,2,0:T(8,128)S(1)}, ...), condition=%wide.region_3.4_spmd.clone.clone, body=%wide.region_2.3_spmd.clone.clone.sunk | while | flops 1078198272 | bytes 330313 | solution.py:125
  17.4 3.6 fusion.266
  21.0 3.6 fusion.266
  24.6 3.6 fusion.266
  28.1 3.6 fusion.266
  35.3 3.6 fusion.266
  42.5 3.6 fusion.266
  46.1 3.6 fusion.266
  53.3 3.6 fusion.266
  66.3 11.6 %add_convert_fusion.2 = bf16[256,768]{1,0:T(8,128)(2,1)S(1)} fusion(f32[256,768]{1,0:T(8,128)S(1)} %copy.51, f32[256,768]{1,0:T(8,128)S(1)} %get-tuple-element.368, f32[768]{0:T(1024)} %get-tuple-element.198, f32[256]{0:T(256)} %get-tuple-element.366, f32[768]{0:T(1024)} %get-tuple-element.199, f32[256]{0:T(256)} %get-tuple-element.365, ...), kind=kLoop, calls=%fused_computation.456 | loop fusion | flops 38338560 | bytes 2231296 | tf_op jit(solution)/shard_map/convert_element_type | solution.py:140
  83.6 11.4 %reduce-scatter.3.cloned.1.call-start = ((), (), s32[]{:S(2)}) async-start(), calls=%async_computation.3 | async-start | bytes 3538944 | tf_op jit(solution)/shard_map/reduce_scatter | solution.py:155
  96.2 53.2 %all-gather.3.cloned.1.call-done = bf16[2048,768]{1,0:T(8,128)(2,1)} async-done(((bf16[256,768]{1,0:T(8,128)(2,1)}), bf16[2048,768]{1,0:T(8,128)(2,1)}) %all-gather.3.cloned.1.call-update) | async-done | bytes 3145744 | tf_op jit(solution)/shard_map/all_gather | solution.py:151
  149.4 11.6 %multiply_convert_fusion = (bf16[2048,384]{1,0:T(8,128)(2,1)S(1)}, f32[2048,384]{1,0:T(8,128)}, f32[2048,384]{1,0:T(8,128)}) fusion(f32[384]{0:T(512)} %convert_element_type.529, bf16[2048,768]{1,0:T(8,128)(2,1)} %all-gather.3.cloned.1.call-done, bf16[768,384]{1,0:T(8,128)(2,1)} %param.29), kind=kOutput, calls=%fused_computation.148 | convolution fusion | flops 1259864064 | bytes 11601408 | tf_op jit(solution)/shard_map/dot_general | solution.py:152
  169.5 72.7 %reduce-scatter.3.cloned.1.call-done = bf16[256,768]{1,0:T(8,128)(2,1)} async-done(((bf16[2048,768]{1,0:T(8,128)(2,1)}), bf16[256,768]{1,0:T(8,128)(2,1)}) %reduce-scatter.3.cloned.1.call-update) | async-done | bytes 393232 | tf_op jit(solution)/shard_map/reduce_scatter | solution.py:155
  249.4 62.5 %all-gather.5.cloned.1.call-done = bf16[2048,768]{1,0:T(8,128)(2,1)} async-done(((bf16[256,768]{1,0:T(8,128)(2,1)}), bf16[2048,768]{1,0:T(8,128)(2,1)}) %all-gather.5.cloned.1.call-update) | async-done | bytes 3145744 | tf_op jit(solution)/shard_map/all_gather | solution.py:167
  311.9 7.3 %fusion.230 = (bf16[384]{0:T(512)(128)(2,1)}, bf16[2048,384]{1,0:T(8,128)(2,1)S(1)}) fusion(f32[2048,384]{1,0:T(8,128)} %get-tuple-element.299, f32[2048,384]{1,0:T(8,128)} %get-tuple-element.373, bf16[2048,768]{1,0:T(8,128)(2,1)} %all-gather.5.cloned.1.call-done, bf16[384,768]{1,0:T(8,128)(2,1)} %param.31), kind=kOutput, calls=%fused_computation.674 | convolution fusion | flops 1219755648 | bytes 11600640 | tf_op jit(solution)/shard_map/dot_general | solution.py:13
  324.0 4.8 convolution_convert_fusion.2
  331.5 69.1 %reduce-scatter.5.cloned.1.call-done = bf16[256,768]{1,0:T(8,128)(2,1)} async-done(((bf16[2048,768]{1,0:T(8,128)(2,1)}), bf16[256,768]{1,0:T(8,128)(2,1)}) %reduce-scatter.5.cloned.1.call-update) | async-done | bytes 393232 | tf_op jit(solution)/shard_map/reduce_scatter | solution.py:173
  451.9 5.8 stack.263
  457.7 11.7 %convert_reduce_fusion.3 = (f32[768]{0:T(1024)S(1)}, bf16[256,768]{1,0:T(8,128)(2,1)S(1)}) fusion(f32[256]{0:T(256)} %copy-done.110, f32[256,768]{1,0:T(8,128)S(1)} %copy.53, f32[768]{0:T(1024)} %get-tuple-element.198, f32[256]{0:T(256)} %get-tuple-element.303, f32[768]{0:T(1024)} %get-tuple-element.199, f32[256]{0:T(256)} %get-tuple-element.321, ...), kind=kLoop, calls=%fused_computation.446 | loop fusion | flops 38927616 | bytes 2235392 | tf_op jit(solution)/shard_map/reduce_sum | solution.py:191
  472.0 28.5 %psum.99 = bf16[384]{0:T(512)(128)(2,1)S(1)} all-reduce(bf16[384]{0:T(512)(128)(2,1)S(1)} %copy-done.120), channel_id=1, replica_groups=mesh['dp'=16,'tensor'=8] {'dp'}, use_global_device_ids=true, to_apply=%region_94.95 | all-reduce | flops 384 | bytes 1536 | tf_op jit(solution)/shard_map/psum | solution.py:197
  501.1 22.6 %all-reduce.11.cloned.1.call-done = (bf16[768,384]{1,0:T(8,128)(2,1)}, bf16[384,768]{1,0:T(8,128)(2,1)}) async-done(((bf16[768,384]{1,0:T(8,128)(2,1)}, bf16[384,768]{1,0:T(8,128)(2,1)}), (bf16[768,384]{1,0:T(8,128)(2,1)}, bf16[384,768]{1,0:T(8,128)(2,1)})) %all-reduce.11.cloned.1.call-update) | async-done | bytes 1179664 | tf_op jit(solution)/shard_map/psum | solution.py:195
  528.0 68.4 %all-reduce.3 = (f32[768]{0:T(1024)}, f32[768]{0:T(1024)}, f32[768]{0:T(1024)}, f32[768]{0:T(1024)}, f32[768]{0:T(1024)}, /*index=5*/f32[768]{0:T(1024)}, f32[768]{0:T(1024)}) all-reduce(f32[768]{0:T(1024)S(1)} %get-tuple-element.290, f32[768]{0:T(1024)S(1)} %copy-done.37, ...), channel_id=1, replica_groups=mesh['dp'=16,'tensor'=8] {'dp','tensor'}, use_global_device_ids=true, to_apply=%region_18.19 | all-reduce | flops 5376 | bytes 43008 | tf_op jit(solution)/shard_map/psum | solution.py:210
  597.9 89.3 %all-reduce.9.cloned.1.call-done = (f32[768,768]{0,1:T(8,128)}, f32[65,768]{1,0:T(8,128)}, f32[768,768]{1,0:T(8,128)}) async-done(((f32[768,768]{0,1:T(8,128)}, f32[65,768]{1,0:T(8,128)}, f32[768,768]{1,0:T(8,128)}), (f32[768,768]{0,1:T(8,128)}, f32[65,768]{1,0:T(8,128)}, f32[768,768]{1,0:T(8,128)})) %all-reduce.9.cloned.1.call-update) | async-done | bytes 4918288 | tf_op jit(solution)/shard_map/psum | solution.py:210
  (413 shorter events, 125.8 us)
Async XLA Ops:
  7.2 53.3 %copy-start = (bf16[768,768]{1,0:T(8,128)(2,1)S(1)}, bf16[768,768]{1,0:T(8,128)(2,1)}, u32[]{:S(2)}) copy-start(bf16[768,768]{1,0:T(8,128)(2,1)} %param.22) | copy-start | bytes 3538948
  7.2 142.2 %all-gather.3.cloned.1.call-start = ((), (), s32[]{:S(2)}) async-start(), calls=%async_computation.2 | async-start | bytes 3538944 | tf_op jit(solution)/shard_map/all_gather | solution.py:151
  17.3 43.1 %copy-start.119 = (s32[256]{0:T(256)S(1)}, s32[256]{0:T(256)}, u32[]{:S(2)}) copy-start(s32[256]{0:T(256)} %param.37) | copy-start | bytes 3076
  17.3 43.1 %copy-start.116 = (bf16[768]{0:T(1024)(128)(2,1)S(1)}, bf16[768]{0:T(1024)(128)(2,1)}, u32[]{:S(2)}) copy-start(bf16[768]{0:T(1024)(128)(2,1)} %param.23) | copy-start | bytes 4612
  17.3 43.1 %copy-start.6 = (bf16[256,768]{1,0:T(8,128)(2,1)S(1)}, bf16[256,768]{1,0:T(8,128)(2,1)}, u32[]{:S(2)}) copy-start(bf16[256,768]{1,0:T(8,128)(2,1)} %param.21) | copy-start | bytes 1179652
  83.6 158.7 %reduce-scatter.3.cloned.1.call-start = ((), (), s32[]{:S(2)}) async-start(), calls=%async_computation.3 | async-start | bytes 3538944 | tf_op jit(solution)/shard_map/reduce_scatter | solution.py:155
  165.6 146.3 %all-gather.5.cloned.1.call-start = ((), (), s32[]{:S(2)}) async-start(), calls=%async_computation.4 | async-start | bytes 3538944 | tf_op jit(solution)/shard_map/all_gather | solution.py:167
  249.3 151.3 %reduce-scatter.5.cloned.1.call-start = ((), (), s32[]{:S(2)}) async-start(), calls=%async_computation.5 | async-start | bytes 3538944 | tf_op jit(solution)/shard_map/reduce_scatter | solution.py:173
  323.9 199.8 %all-reduce.11.cloned.1.call-start = ((), (), s32[]{:S(2)}) async-start(), calls=%async_computation.7 | async-start | bytes 2359296 | tf_op jit(solution)/shard_map/psum | solution.py:195
  331.4 355.7 %all-reduce.9.cloned.1.call-start = ((), (), s32[]{:S(2)}) async-start(), calls=%async_computation.6 | async-start | bytes 9879552 | tf_op jit(solution)/shard_map/psum | solution.py:210
  429.2 21.2 %copy-start.42 = (f32[768]{0:T(1024)S(1)}, f32[768]{0:T(1024)}, u32[]{:S(2)}) copy-start(f32[768]{0:T(1024)} %get-tuple-element.186) | copy-start | bytes 9220
  429.2 21.2 %copy-start.41 = (f32[768]{0:T(1024)S(1)}, f32[768]{0:T(1024)}, u32[]{:S(2)}) copy-start(f32[768]{0:T(1024)} %get-tuple-element.185) | copy-start | bytes 9220
  429.2 21.3 %copy-start.40 = (f32[768]{0:T(1024)S(1)}, f32[768]{0:T(1024)}, u32[]{:S(2)}) copy-start(f32[768]{0:T(1024)} %get-tuple-element.184) | copy-start | bytes 9220
  429.2 21.3 %copy-start.39 = (f32[768]{0:T(1024)S(1)}, f32[768]{0:T(1024)}, u32[]{:S(2)}) copy-start(f32[768]{0:T(1024)} %get-tuple-element.183) | copy-start | bytes 9220
  429.2 21.3 %copy-start.38 = (f32[768]{0:T(1024)S(1)}, f32[768]{0:T(1024)}, u32[]{:S(2)}) copy-start(f32[768]{0:T(1024)} %get-tuple-element.182) | copy-start | bytes 9220
  430.6 38.8 %copy-start.7 = (bf16[256,768]{1,0:T(8,128)(2,1)S(1)}, bf16[256,768]{1,0:T(8,128)(2,1)}, u32[]{:S(2)}) copy-start(bf16[256,768]{1,0:T(8,128)(2,1)} %param.21) | copy-start | bytes 1179652
  471.3 56.7 %copy-start.32 = (f32[768]{0:T(1024)S(1)}, f32[768]{0:T(1024)}, u32[]{:S(2)}) copy-start(f32[768]{0:T(1024)} %get-tuple-element.193) | copy-start | bytes 9220
  471.3 56.7 %copy-start.33 = (f32[768]{0:T(1024)S(1)}, f32[768]{0:T(1024)}, u32[]{:S(2)}) copy-start(f32[768]{0:T(1024)} %get-tuple-element.196) | copy-start | bytes 9220
  471.3 56.7 %copy-start.34 = (f32[768]{0:T(1024)S(1)}, f32[768]{0:T(1024)}, u32[]{:S(2)}) copy-start(f32[768]{0:T(1024)} %get-tuple-element.286) | copy-start | bytes 9220
  471.3 56.7 %copy-start.35 = (f32[768]{0:T(1024)S(1)}, f32[768]{0:T(1024)}, u32[]{:S(2)}) copy-start(f32[768]{0:T(1024)} %get-tuple-element.126) | copy-start | bytes 9220
  471.3 56.7 %copy-start.36 = (f32[768]{0:T(1024)S(1)}, f32[768]{0:T(1024)}, u32[]{:S(2)}) copy-start(f32[768]{0:T(1024)} %get-tuple-element.195) | copy-start | bytes 9220
  471.4 56.7 %copy-start.37 = (f32[768]{0:T(1024)S(1)}, f32[768]{0:T(1024)}, u32[]{:S(2)}) copy-start(f32[768]{0:T(1024)} %get-tuple-element.288) | copy-start | bytes 9220
  471.4 125.1 %copy-start.3 = (f32[256,768]{1,0:T(8,128)S(1)}, f32[256,768]{1,0:T(8,128)}, u32[]{:S(2)}) copy-start(f32[256,768]{1,0:T(8,128)} %copy-done.2) | copy-start | bytes 2359300
  471.4 125.1 %copy-start.115 = (f32[256]{0:T(256)S(1)}, f32[256]{0:T(256)}, u32[]{:S(2)}) copy-start(f32[256]{0:T(256)} %copy-done.114) | copy-start | bytes 3076
  (106 other events, 1160.3 us)
Sparse Core Ops, SparseCore 0:
  83.7 65.6 all-gather.2
  165.7 76.4 reduce-scatter.2
  249.5 62.4 all-gather.4
  324.0 76.5 reduce-scatter.4
  403.6 120.0 all-reduce.10
  529.7 157.4 all-reduce.8
where the time goes:
time: 710 us; the launch traced here: 701 us
  waiting for transfers between devices  369 us (52%)
  blocking collectives  97 us (14%)
  matrix products  88.4 us (12%)
  other arithmetic  70.4 us (10%)
  local copies, waits for them, and re-layouts  48.2 us (7%)
  between operations  16.4 us (2%)
  starting transfers between devices  11.6 us (2%)
    psum x1, waiting for transfers between devices, body(): lax.psum((grad_w_value, grad_b_value, grad_kernel, grad_w_out, grad_b_out...  89.3 us
    reduce_scatter x1, waiting for transfers between devices, body(): lax.psum_scatter(jnp.dot(active, w_down, preferred_element_type=jnp.float...  72.7 us
    reduce_scatter x1, waiting for transfers between devices, body(): lax.psum_scatter(dot_last(upper_grad, w_up).astype(jnp.bfloat16), 'tensor...  69.1 us
    psum x1, blocking collectives, body(): lax.psum((grad_w_value, grad_b_value, grad_kernel, grad_w_out, grad_b_out...  68.4 us
    all_gather x1, waiting for transfers between devices, body(): grad_rows_all = lax.all_gather(branch_grad, 'tensor', axis=0, tiled=True)  62.5 us
    dot_general x16, matrix products, dot_last(): lax.dot_general(former, latter, (((1,), (1,)), ((), ())), preferred_eleme...  56.4 us
    all_gather x1, waiting for transfers between devices, body(): gathered = lax.all_gather(first_low, 'tensor', axis=0, tiled=True)  53.2 us
    psum x1, blocking collectives, body(): lax.psum(grad_b_up.astype(jnp.bfloat16), 'dp').astype(jnp.float32)  28.5 us
  transfers between devices with their start and end apart: 6, of which 6 were waited for; matrix products, arithmetic and copies ran while one was open for 12% of the time, Pallas kernels for 0%

commit v1 on v0

--- a/solution.py
+++ b/solution.py
@@ -7,6 +7,9 @@
 HEADS = 12
 SETS = 32
 BUCKETS = 256
+unite_matrix_over_axis = lambda obj, axis_id, device_axis: lax.psum(
+    lax.psum(obj, axis_id), device_axis
+)
 
 
 def dot_last(former, latter):
@@ -207,7 +210,7 @@
         grad_b_down,
         grad_gain_ffn,
         grad_shift_ffn,
-    ) = lax.psum(
+    ) = unite_matrix_over_axis(
         (
             grad_w_value,
             grad_b_value,
@@ -220,7 +223,8 @@
             grad_gain_ffn,
             grad_shift_ffn,
         ),
-        ("dp", "tensor"),
+        "dp",
+        "tensor",
     )
     return (
         block_output.astype(jnp.bfloat16),

time: 710 us -> 902 us (1.27)
  waiting for transfers between devices: 369 us -> 523 us
  blocking collectives: 97 us -> 123 us
  local copies, waits for them, and re-layouts: 48.2 us -> 70.4 us
  starting transfers between devices: 11.6 us -> 1.14 us
    psum x1, waiting for transfers between devices: 22.6 us -> 96.7 us  [body(): lax.psum(grad_w_up.astype(jnp.bfloat16), 'dp').astype(jnp.float32)]
    psum x1 -> x2, waiting for transfers between devices: 89.3 us -> 150 us  [the longest x1 124 us: lax.psum(obj, axis_id)]
    psum x1 -> x2, blocking collectives: 68.4 us -> 95.3 us  [the longest x1 55.1 us: lax.psum(obj, axis_id)]
    another operation x66, local copies, waits for them, and re-layouts: 25 us -> 48 us  [conv_back(): return (value_grad, jnp.stack(tap_rows, axis=0))]
    all_gather x1, waiting for transfers between devices: 53.2 us -> 64 us  [body(): gathered = lax.all_gather(first_low, 'tensor', axis=0, tiled=True)]
    reduce_scatter x1, starting transfers between devices: 11.4 us -> 0.51 us  [body(): lax.psum_scatter(jnp.dot(active, w_down, preferred_element_type=jnp.float...]
  transfers between devices with their start and end apart: 6 -> 7, of which waited for: 6 -> 7; matrix products, arithmetic and copies ran while one was open for 12% -> 2% of each run, Pallas kernels for 0% -> 0%
where the time goes in v1:
time: 902 us; the launch traced here: 892 us
  waiting for transfers between devices  523 us (58%)
  blocking collectives  123 us (14%)
  matrix products  88.3 us (10%)
  other arithmetic  70.7 us (8%)
  local copies, waits for them, and re-layouts  70.4 us (8%)
  between operations  15.4 us (2%)
    psum x1, waiting for transfers between devices, lax.psum(obj, axis_id)  124 us
    psum x1, waiting for transfers between devices, body(): lax.psum(grad_w_up.astype(jnp.bfloat16), 'dp').astype(jnp.float32)  96.7 us
    reduce_scatter x1, waiting for transfers between devices, body(): lax.psum_scatter(dot_last(upper_grad, w_up).astype(jnp.bfloat16), 'tensor...  76.5 us
    reduce_scatter x1, waiting for transfers between devices, body(): lax.psum_scatter(jnp.dot(active, w_down, preferred_element_type=jnp.float...  72.7 us
    all_gather x1, waiting for transfers between devices, body(): gathered = lax.all_gather(first_low, 'tensor', axis=0, tiled=True)  64 us
    all_gather x1, waiting for transfers between devices, body(): grad_rows_all = lax.all_gather(branch_grad, 'tensor', axis=0, tiled=True)  62.5 us
    dot_general x16, matrix products, dot_last(): lax.dot_general(former, latter, (((1,), (1,)), ((), ())), preferred_eleme...  56.4 us
    psum x1, blocking collectives, lax.psum(obj, axis_id)  55.1 us
  transfers between devices with their start and end apart: 7, of which 7 were waited for; matrix products, arithmetic and copies ran while one was open for 2% of the time, Pallas kernels for 0%

profile of v1, /device:TPU:1, one launch (start us, length us, event | category | flops | bytes accessed | tf_op | source)
XLA Modules:
  0.0 892.1 jit_solution(2533941319769814438)
XLA Ops:
  17.3 43.1 %while.12 = (s32[]{:T(128)}, bf16[12,256,256]{2,1,0:T(8,128)(2,1)}, s32[12,256,32]{1,2,0:T(8,128)S(1)}, s32[12,256,32]{1,2,0:T(8,128)S(1)}, s32[256]{0:T(256)S(1)}, /*index=5*/s32[]{:T(128)}) while((s32[]{:T(128)}, bf16[12,256,256]{2,1,0:T(8,128)(2,1)}, s32[12,256,32]{1,2,0:T(8,128)S(1)}, s32[12,256,32]{1,2,0:T(8,128)S(1)}, ...), condition=%wide.region_3.4_spmd.clone.clone, body=%wide.region_2.3_spmd.clone.clone.sunk | while | flops 1078198272 | bytes 330313 | solution.py:128
  17.4 3.6 fusion.266
  24.5 3.6 fusion.266
  28.1 3.6 fusion.266
  35.3 3.6 fusion.266
  42.5 3.6 fusion.266
  49.7 3.6 fusion.266
  53.2 3.6 fusion.266
  66.3 11.6 %add_convert_fusion.2 = bf16[256,768]{1,0:T(8,128)(2,1)S(1)} fusion(f32[256,768]{1,0:T(8,128)S(1)} %copy.51, f32[256,768]{1,0:T(8,128)S(1)} %get-tuple-element.378, f32[768]{0:T(1024)} %get-tuple-element.198, f32[256]{0:T(256)} %get-tuple-element.376, f32[768]{0:T(1024)} %get-tuple-element.199, f32[256]{0:T(256)} %get-tuple-element.375, ...), kind=kLoop, calls=%fused_computation.456 | loop fusion | flops 38338560 | bytes 2231296 | tf_op jit(solution)/shard_map/convert_element_type | solution.py:143
  85.4 64.0 %all-gather.3.cloned.1.call-done = bf16[2048,768]{1,0:T(8,128)(2,1)} async-done(((bf16[256,768]{1,0:T(8,128)(2,1)}), bf16[2048,768]{1,0:T(8,128)(2,1)}) %all-gather.3.cloned.1.call-update) | async-done | bytes 3145744 | tf_op jit(solution)/shard_map/all_gather | solution.py:154
  149.4 11.5 %multiply_convert_fusion = (bf16[2048,384]{1,0:T(8,128)(2,1)S(1)}, f32[2048,384]{1,0:T(8,128)}, f32[2048,384]{1,0:T(8,128)}) fusion(f32[384]{0:T(512)} %convert_element_type.529, bf16[2048,768]{1,0:T(8,128)(2,1)} %all-gather.3.cloned.1.call-done, bf16[768,384]{1,0:T(8,128)(2,1)} %param.29), kind=kOutput, calls=%fused_computation.148 | convolution fusion | flops 1259864064 | bytes 11601408 | tf_op jit(solution)/shard_map/dot_general | solution.py:155
  169.5 72.7 %reduce-scatter.3.cloned.1.call-done = bf16[256,768]{1,0:T(8,128)(2,1)} async-done(((bf16[2048,768]{1,0:T(8,128)(2,1)}), bf16[256,768]{1,0:T(8,128)(2,1)}) %reduce-scatter.3.cloned.1.call-update) | async-done | bytes 393232 | tf_op jit(solution)/shard_map/reduce_scatter | solution.py:158
  249.4 62.5 %all-gather.5.cloned.1.call-done = bf16[2048,768]{1,0:T(8,128)(2,1)} async-done(((bf16[256,768]{1,0:T(8,128)(2,1)}), bf16[2048,768]{1,0:T(8,128)(2,1)}) %all-gather.5.cloned.1.call-update) | async-done | bytes 3145744 | tf_op jit(solution)/shard_map/all_gather | solution.py:170
  311.9 7.3 fusion.230
  324.2 76.5 %reduce-scatter.5.cloned.1.call-done = bf16[256,768]{1,0:T(8,128)(2,1)} async-done(((bf16[2048,768]{1,0:T(8,128)(2,1)}), bf16[256,768]{1,0:T(8,128)(2,1)}) %reduce-scatter.5.cloned.1.call-update) | async-done | bytes 393232 | tf_op jit(solution)/shard_map/reduce_scatter | solution.py:176
  431.6 12.1 %convert_reduce_fusion.3 = (f32[768]{0:T(1024)S(1)}, bf16[256,768]{1,0:T(8,128)(2,1)S(1)}) fusion(f32[256]{0:T(256)} %copy-done.76, f32[256,768]{1,0:T(8,128)S(1)} %copy.53, f32[768]{0:T(1024)} %get-tuple-element.198, f32[256]{0:T(256)} %get-tuple-element.313, f32[768]{0:T(1024)} %get-tuple-element.199, f32[256]{0:T(256)} %get-tuple-element.331, ...), kind=kLoop, calls=%fused_computation.446 | loop fusion | flops 38927616 | bytes 2235392 | tf_op jit(solution)/shard_map/reduce_sum | solution.py:194
  487.9 5.8 stack.263
  494.0 4.7 convolution_convert_fusion.2
  501.4 123.5 %all-reduce.12.cloned.1.call-done = (f32[768,768]{0,1:T(8,128)}, f32[65,768]{1,0:T(8,128)}, f32[768,768]{1,0:T(8,128)}) async-done(((f32[768,768]{0,1:T(8,128)}, f32[65,768]{1,0:T(8,128)}, f32[768,768]{1,0:T(8,128)}), (f32[768,768]{0,1:T(8,128)}, f32[65,768]{1,0:T(8,128)}, f32[768,768]{1,0:T(8,128)})) %all-reduce.12.cloned.1.call-update) | async-done | bytes 4918288 | tf_op jit(solution)/shard_map/psum | solution.py:11
  625.0 28.0 %psum.176 = bf16[384]{0:T(512)(128)(2,1)S(1)} all-reduce(bf16[384]{0:T(512)(128)(2,1)S(1)} %copy-done.86), channel_id=1, replica_groups=mesh['dp'=16,'tensor'=8] {'dp'}, use_global_device_ids=true, to_apply=%region_101.102 | all-reduce | flops 384 | bytes 1536 | tf_op jit(solution)/shard_map/psum | solution.py:200
  653.6 96.7 %all-reduce.16.cloned.1.call-done = (bf16[768,384]{1,0:T(8,128)(2,1)}, bf16[384,768]{1,0:T(8,128)(2,1)}) async-done(((bf16[768,384]{1,0:T(8,128)(2,1)}, bf16[384,768]{1,0:T(8,128)(2,1)}), (bf16[768,384]{1,0:T(8,128)(2,1)}, bf16[384,768]{1,0:T(8,128)(2,1)})) %all-reduce.16.cloned.1.call-update) | async-done | bytes 1179664 | tf_op jit(solution)/shard_map/psum | solution.py:198
  754.7 55.1 %all-reduce.3 = (f32[768]{0:T(1024)S(1)}, f32[768]{0:T(1024)S(1)}, f32[768]{0:T(1024)S(1)}, f32[768]{0:T(1024)S(1)}, f32[768]{0:T(1024)S(1)}, /*index=5*/f32[768]{0:T(1024)S(1)}, f32[768]{0:T(1024)S(1)}) all-reduce(f32[768]{0:T(1024)S(1)} %get-tuple-element.300, f32[768]{0:T(1024)S(1)} %copy-done.37, ...), channel_id=1, replica_groups=mesh['dp'=16,'tensor'=8] {'dp'}, use_global_device_ids=true, to_apply=%region_19.20 | all-reduce | flops 5376 | bytes 43008 | tf_op jit(solution)/shard_map/psum | solution.py:11
  809.9 40.2 %all-reduce.5 = (f32[768]{0:T(1024)}, f32[768]{0:T(1024)}, f32[768]{0:T(1024)}, f32[768]{0:T(1024)}, f32[768]{0:T(1024)}, /*index=5*/f32[768]{0:T(1024)}, f32[768]{0:T(1024)}) all-reduce(f32[768]{0:T(1024)S(1)} %get-tuple-element.272, f32[768]{0:T(1024)S(1)} %get-tuple-element.273, ...), channel_id=1, replica_groups=mesh['dp'=16,'tensor'=8] {'tensor'}, use_global_device_ids=true, to_apply=%region_20.21 | all-reduce | flops 5376 | bytes 43008 | tf_op jit(solution)/shard_map/psum | solution.py:10
  851.4 26.6 %all-reduce.14.cloned.1.call-done = (f32[768,768]{0,1:T(8,128)}, f32[65,768]{1,0:T(8,128)}, f32[768,768]{1,0:T(8,128)}) async-done(((f32[768,768]{0,1:T(8,128)}, f32[65,768]{1,0:T(8,128)}, f32[768,768]{1,0:T(8,128)}), (f32[768,768]{0,1:T(8,128)}, f32[65,768]{1,0:T(8,128)}, f32[768,768]{1,0:T(8,128)})) %all-reduce.14.cloned.1.call-update) | async-done | bytes 4918288 | tf_op jit(solution)/shard_map/psum | solution.py:10
  (349 shorter events, 152.5 us)
Async XLA Ops:
  7.2 53.3 %copy-start = (bf16[768,768]{1,0:T(8,128)(2,1)S(1)}, bf16[768,768]{1,0:T(8,128)(2,1)}, u32[]{:S(2)}) copy-start(bf16[768,768]{1,0:T(8,128)(2,1)} %param.22) | copy-start | bytes 3538948
  7.2 142.2 %all-gather.3.cloned.1.call-start = ((), (), s32[]{:S(2)}) async-start(), calls=%async_computation.2 | async-start | bytes 3538944 | tf_op jit(solution)/shard_map/all_gather | solution.py:154
  17.3 43.1 %copy-start.85 = (s32[256]{0:T(256)S(1)}, s32[256]{0:T(256)}, u32[]{:S(2)}) copy-start(s32[256]{0:T(256)} %param.37) | copy-start | bytes 3076
  17.3 43.1 %copy-start.82 = (bf16[768]{0:T(1024)(128)(2,1)S(1)}, bf16[768]{0:T(1024)(128)(2,1)}, u32[]{:S(2)}) copy-start(bf16[768]{0:T(1024)(128)(2,1)} %param.23) | copy-start | bytes 4612
  17.3 43.1 %copy-start.6 = (bf16[256,768]{1,0:T(8,128)(2,1)S(1)}, bf16[256,768]{1,0:T(8,128)(2,1)}, u32[]{:S(2)}) copy-start(bf16[256,768]{1,0:T(8,128)(2,1)} %param.21) | copy-start | bytes 1179652
  83.6 158.7 %reduce-scatter.3.cloned.1.call-start = ((), (), s32[]{:S(2)}) async-start(), calls=%async_computation.3 | async-start | bytes 3538944 | tf_op jit(solution)/shard_map/reduce_scatter | solution.py:158
  165.6 146.3 %all-gather.5.cloned.1.call-start = ((), (), s32[]{:S(2)}) async-start(), calls=%async_computation.4 | async-start | bytes 3538944 | tf_op jit(solution)/shard_map/all_gather | solution.py:170
  249.4 151.3 %reduce-scatter.5.cloned.1.call-start = ((), (), s32[]{:S(2)}) async-start(), calls=%async_computation.5 | async-start | bytes 3538944 | tf_op jit(solution)/shard_map/reduce_scatter | solution.py:176
  323.9 301.0 %all-reduce.12.cloned.1.call-start = ((), (), s32[]{:S(2)}) async-start(), calls=%async_computation.6 | async-start | bytes 9879552 | tf_op jit(solution)/shard_map/psum | solution.py:11
  430.1 54.4 %copy-start.40 = (f32[768]{0:T(1024)S(1)}, f32[768]{0:T(1024)}, u32[]{:S(2)}) copy-start(f32[768]{0:T(1024)} %get-tuple-element.184) | copy-start | bytes 9220
  430.1 54.4 %copy-start.39 = (f32[768]{0:T(1024)S(1)}, f32[768]{0:T(1024)}, u32[]{:S(2)}) copy-start(f32[768]{0:T(1024)} %get-tuple-element.183) | copy-start | bytes 9220
  430.1 54.5 %copy-start.38 = (f32[768]{0:T(1024)S(1)}, f32[768]{0:T(1024)}, u32[]{:S(2)}) copy-start(f32[768]{0:T(1024)} %get-tuple-element.182) | copy-start | bytes 9220
  430.1 55.8 %copy-start.7 = (bf16[256,768]{1,0:T(8,128)(2,1)S(1)}, bf16[256,768]{1,0:T(8,128)(2,1)}, u32[]{:S(2)}) copy-start(bf16[256,768]{1,0:T(8,128)(2,1)} %param.21) | copy-start | bytes 1179652
  493.7 256.7 %all-reduce.16.cloned.1.call-start = ((), (), s32[]{:S(2)}) async-start(), calls=%async_computation.8 | async-start | bytes 2359296 | tf_op jit(solution)/shard_map/psum | solution.py:198
  501.4 123.7 %copy-start.86 = (bf16[384]{0:T(512)(128)(2,1)S(1)}, bf16[384]{0:T(512)(128)(2,1)}, u32[]{:S(2)}) copy-start(bf16[384]{0:T(512)(128)(2,1)} %get-tuple-element.294) | copy-start | bytes 2308
  501.4 376.6 %all-reduce.14.cloned.1.call-start = ((), (), s32[]{:S(2)}) async-start(), calls=%async_computation.7 | async-start | bytes 9879552 | tf_op jit(solution)/shard_map/psum | solution.py:10
  625.0 129.7 %copy-start.32 = (f32[768]{0:T(1024)S(1)}, f32[768]{0:T(1024)}, u32[]{:S(2)}) copy-start(f32[768]{0:T(1024)} %get-tuple-element.193) | copy-start | bytes 9220
  625.0 129.7 %copy-start.33 = (f32[768]{0:T(1024)S(1)}, f32[768]{0:T(1024)}, u32[]{:S(2)}) copy-start(f32[768]{0:T(1024)} %get-tuple-element.196) | copy-start | bytes 9220
  625.0 129.7 %copy-start.34 = (f32[768]{0:T(1024)S(1)}, f32[768]{0:T(1024)}, u32[]{:S(2)}) copy-start(f32[768]{0:T(1024)} %get-tuple-element.296) | copy-start | bytes 9220
  625.0 129.7 %copy-start.35 = (f32[768]{0:T(1024)S(1)}, f32[768]{0:T(1024)}, u32[]{:S(2)}) copy-start(f32[768]{0:T(1024)} %get-tuple-element.126) | copy-start | bytes 9220
  625.0 129.7 %copy-start.36 = (f32[768]{0:T(1024)S(1)}, f32[768]{0:T(1024)}, u32[]{:S(2)}) copy-start(f32[768]{0:T(1024)} %get-tuple-element.195) | copy-start | bytes 9220
  625.0 129.7 %copy-start.37 = (f32[768]{0:T(1024)S(1)}, f32[768]{0:T(1024)}, u32[]{:S(2)}) copy-start(f32[768]{0:T(1024)} %get-tuple-element.298) | copy-start | bytes 9220
  625.0 225.1 %copy-start.3 = (f32[256,768]{1,0:T(8,128)S(1)}, f32[256,768]{1,0:T(8,128)}, u32[]{:S(2)}) copy-start(f32[256,768]{1,0:T(8,128)} %copy-done.2) | copy-start | bytes 2359300
  625.0 225.1 %copy-start.81 = (f32[256]{0:T(256)S(1)}, f32[256]{0:T(256)}, u32[]{:S(2)}) copy-start(f32[256]{0:T(256)} %copy-done.80) | copy-start | bytes 3076
  (73 other events, 482.8 us)
Sparse Core Ops, SparseCore 0:
  83.7 65.6 all-gather.2
  165.8 76.4 reduce-scatter.2
  249.5 62.4 all-gather.4
  324.1 76.5 reduce-scatter.4
  493.8 131.1 all-reduce.11
  628.7 121.6 all-reduce.15
  753.4 124.6 all-reduce.13
